TPU v7x, 32 devices: a whole 2x2x4 slice. The times are simulated.
32 devices in a mesh: kpt: 2 (over x), orb: 16 (over z, y, core).
Axes of the slice: x: 2, y: 2, z: 4, core: 2. Of those that a mesh axis runs over, the one named last changes fastest.
Arguments:
- wavefunctions: float32 [2, 48, 102400], P('kpt', 'orb'), may hold values from -8 to 8
- kpoint_vector: float32 [2, 3], P('kpt'), may hold values from -1 to 1
- kpoint_weight: float32 [2], P('kpt'), may hold values from 0.05 to 0.3
- occupation: float32 [48], replicated, may hold values from 0.25 to 2
- orbital_slot: int32 [48], replicated, may hold values from 0 to 47, as said below
- piece_rows: int32 [16], replicated, may hold values from 1 to 80, 640 in all
- external_potential: float32 [8, 6400], P(None, 'orb'), may hold values from -6 to 6
- core_density: float32 [8, 6400], P(None, 'orb'), may hold values from 0.1 to 4
Outputs:
- density: float32 [8, 6400], P(None, 'orb')
- new_orbitals: float32 [2, 48, 204800], P('kpt', None, 'orb')
Inputs may be any that keep to these rules, and one draw needn't show every extreme that they name: `orbital_slot`: distinct slot numbers; 0 and 47 are always among them. `piece_rows`: the entries sum to 640.
All inputs are finite; a program needn't handle non-finite values.
Results may differ from a plain program's by a relative error of at most 0.00013.
Values sent between devices are 32-bit elements; how exact they have to be, the bound alone decides.
A program may use at most 64 MiB of HBM per device.

v0:
```python
import functools
import math

import jax
import jax.numpy as jnp
import numpy as np
from jax import lax
from jax.experimental import pallas as pl
from jax.experimental.pallas import tpu as pltpu
from jax.sharding import PartitionSpec as P

NX = 80
NY = 80
NZ = 8


magic_taps = (
    8.433424733352934e-07,
    -1.290557201342061e-05,
    8.76298447621056e-05,
    -0.00030158038132690465,
    0.001747237136729939,
    -0.009420470302010804,
    0.023738214637249424,
    0.0612625895831208,
    0.9940415697834004,
    -0.06048952891969835,
    -0.021030251609303816,
    0.013372634148547948,
    -0.0034412814449349387,
    0.0004944322768868992,
    -5.185986881173433e-05,
    2.7273449291197967e-06,
)
grid_step = 0.9
half_order = 14
spectrum_center = 13.0
spectrum_half = 17.0
exchange_coef = (3.0 / math.pi) ** (1.0 / 3.0)
exact_mode = lax.Precision.HIGHEST


def stencil_taps():
    factorial = math.factorial
    second_taps = {}
    first_taps = {}
    running = 0.0
    for offset in range(1, half_order + 1):
        weight_j = factorial(half_order) ** 2 / (
            factorial(half_order - offset) * factorial(half_order + offset)
        )
        tap_sign = (-1.0) ** (offset + 1)
        second_taps[offset] = 2.0 * tap_sign * weight_j / offset**2
        second_taps[-offset] = second_taps[offset]
        first_taps[offset] = tap_sign * weight_j / offset
        first_taps[-offset] = -first_taps[offset]
        running = running + 2.0 * second_taps[offset]
    second_taps[0] = -running
    return (second_taps, first_taps)


def band_matrix(length, taps):
    matrix = np.zeros((length, length))
    for offset, tap_value in taps.items():
        matrix = matrix + tap_value * np.eye(length, k=offset)
    return matrix


def axis_tables(length):
    second_taps, first_taps = stencil_taps()
    magic_band = band_matrix(
        length, {tap_index - 8: magic_taps[tap_index] for tap_index in range(16)}
    )
    return (
        band_matrix(length, second_taps) * (-0.5 / grid_step**2),
        band_matrix(length, first_taps) / grid_step,
        magic_band,
    )


MESH = pl.DeviceIdType.MESH
BF = jnp.bfloat16
VMEM = pl.BlockSpec(memory_space=pltpu.VMEM)
SMEM = pl.BlockSpec(memory_space=pltpu.SMEM)


def split(x):
    high = x.astype(BF)
    return high, (x - high.astype(jnp.float32)).astype(BF)


def split_table(x):
    high = x.astype(BF)
    return high, (x - high.astype(np.float32)).astype(BF)


def dot(a, b):
    return lax.dot_general(a, b, (((1,), (0,)), ((), ())), preferred_element_type=jnp.float32)


def dot_nt(a, b):
    return lax.dot_general(a, b, (((1,), (1,)), ((), ())), preferred_element_type=jnp.float32)


def mm(ah, al, bh, bl):
    return dot(ah, bh) + dot(ah, bl) + dot(al, bh)


def swap_lanes(x, slots):
    parts = []
    for s in range(slots):
        parts += [x[:, (2 * s + 1) * NX:(2 * s + 2) * NX], -x[:, 2 * s * NX:(2 * s + 1) * NX]]
    return jnp.concatenate(parts, axis=1)


def put_split(refs, at, x):
    high, low = split(x)
    refs[0][at, :] = high
    refs[1][at, :] = low


def tables(slots, wave_vector):
    d2, d1, magic = axis_tables(NX)
    d2z, d1z, magic_z = axis_tables(NZ)
    d2y, d1y, magic_y = axis_tables(NY)
    f = lambda m: np.asarray(m, np.float32)
    wide = lambda m: f(np.tile(m, (1, NZ)))
    tall = lambda m: f(np.repeat(m, NY, axis=1))
    eye = np.eye(2 * slots)
    magic_x = split_table(f(np.kron(eye, magic.T)))
    magic_xt = split_table(f(np.kron(eye, magic)))
    twist = np.array([[0.0, 1.0], [-1.0, 0.0]])
    along_x = (
        jnp.asarray(f(np.kron(eye, d2.T)))
        + wave_vector[0] * jnp.asarray(f(np.kron(np.eye(slots), np.kron(twist, d1).T)))
        + 0.5 * jnp.sum(wave_vector * wave_vector) * jnp.eye(2 * slots * NX, dtype=jnp.float32)
    )
    first = [wide(magic_y), tall(magic_z)]
    second = [
        wide(magic_y.T), tall(magic_z.T),
        wide(d2y), tall(np.eye(NZ)), wide(np.eye(NY)), tall(d2z),
        wave_vector[1] * jnp.asarray(wide(d1y)), wave_vector[2] * jnp.asarray(tall(d1z)),
    ]
    return first, second, magic_x, magic_xt, along_x


def tiles_of(rows, tile, body):
    def step(t, carry):
        body(pl.ds(pl.multiple_of(t * tile, tile), tile))
        return carry

    lax.fori_loop(0, rows // tile, step, 0)


TILE = 320


def smooth_kernel(slots, v_ref, my, mz, mxh, mxl, w_ref, smooth_ref, part_ref, mh_out, ml_out,
                  th, tl, dens):
    rows = NZ * NY
    for z in range(NZ):
        block = my[...] * mz[z:z + 1, :]
        put_split((mh_out, ml_out), pl.ds(z * NY, NY), block)

    def along(at):
        vh, vl = split(v_ref[at, :])
        put_split((th, tl), at, mm(vh, vl, mxh[...], mxl[...]))

    tiles_of(rows, TILE, along)

    def across(at):
        s = mm(mh_out[at, :], ml_out[at, :], th[...], tl[...])
        smooth_ref[at, :] = s
        q = s * s * w_ref[...]
        total = q[:, :NX]
        for i in range(1, 2 * slots):
            total = total + q[:, i * NX:(i + 1) * NX]
        dens[at, :] = total

    tiles_of(rows, TILE, across)
    group = 8
    for g in range(NY // group):
        part_ref[:, g * group * NX:(g + 1) * group * NX] = jnp.concatenate(
            [dens[pl.ds(g * group + y, NZ, stride=NY), :] for y in range(group)], axis=1
        )


def density_kernel(kpts, ranks, part_ref, ext_ref, core_ref, dens_ref, pot_ref,
                   send1, recv1, send2, recv2, own_d, recv_d, s1, r1, s2, r2, s3, r3):
    k = lax.axis_index("kpt")
    o = lax.axis_index("orb")
    every = kpts * ranks
    me = k * ranks + o
    planes = NZ // kpts
    width = ext_ref.shape[1]
    barrier = pltpu.get_barrier_semaphore()

    def peer(i):
        d = lax.rem(me + i, every)
        return d, d // ranks, lax.rem(d, ranks)

    def greet(i, c):
        _, dk, do = peer(i)
        pl.semaphore_signal(barrier, inc=1, device_id=(dk, do), device_id_type=MESH)
        return c

    lax.fori_loop(1, every, greet, 0)
    for j in range(every):
        a, b = divmod(j, ranks)
        send1[j] = part_ref[a * planes:(a + 1) * planes, b * width:(b + 1) * width]
    pl.semaphore_wait(barrier, every - 1)

    def copy1(i):
        d, dk, do = peer(i)
        return pltpu.make_async_remote_copy(
            src_ref=send1.at[d], dst_ref=recv1.at[me], send_sem=s1.at[d], recv_sem=r1.at[me],
            device_id=(dk, do), device_id_type=MESH)

    def copy2(i):
        d, dk, do = peer(i)
        return pltpu.make_async_remote_copy(
            src_ref=send2, dst_ref=recv2.at[me], send_sem=s2.at[d], recv_sem=r2.at[me],
            device_id=(dk, do), device_id_type=MESH)

    def copy3(i):
        dk = lax.rem(k + i, kpts)
        return pltpu.make_async_remote_copy(
            src_ref=own_d, dst_ref=recv_d.at[k], send_sem=s3.at[dk], recv_sem=r3.at[k],
            device_id=(dk, o), device_id_type=MESH)

    def arrived(i, buf, sends, recvs):
        d, dk, do = peer(i)
        return pltpu.make_async_remote_copy(
            src_ref=buf.at[d], dst_ref=buf.at[d], send_sem=sends.at[d], recv_sem=recvs.at[d],
            device_id=(dk, do), device_id_type=MESH)

    def loop(f):
        def step(i, c):
            f(i)
            return c
        lax.fori_loop(1, every, step, 0)

    loop(lambda i: copy1(i).start())
    recv1[me] = send1[me]
    loop(lambda i: arrived(i, recv1, s1, r1).wait_recv())
    total = recv1[0]
    for j in range(1, every):
        total = total + recv1[j]
    own_d[...] = total
    recv_d[k] = total

    def own_planes(ref):
        picked = ref[:planes, :]
        for a in range(1, kpts):
            picked = jnp.where(k == a, ref[a * planes:(a + 1) * planes, :], picked)
        return picked

    level = total + own_planes(core_ref)
    value = own_planes(ext_ref) - exchange_coef * jnp.exp(jnp.log(level) * (1.0 / 3.0))
    send2[...] = value
    recv2[me] = value
    loop(lambda i: copy2(i).start())
    for i in range(1, kpts):
        copy3(i).start()
    loop(lambda i: arrived(i, recv2, s2, r2).wait_recv())
    for j in range(every):
        a, b = divmod(j, ranks)
        pot_ref[a * planes:(a + 1) * planes, b * width:(b + 1) * width] = recv2[j]
    for i in range(1, kpts):
        dk = lax.rem(k + i, kpts)
        pltpu.make_async_remote_copy(
            src_ref=own_d, dst_ref=recv_d.at[dk], send_sem=s3.at[dk], recv_sem=r3.at[dk],
            device_id=(dk, o), device_id_type=MESH).wait_recv()
    for a in range(kpts):
        dens_ref[a * planes:(a + 1) * planes, :] = recv_d[a]
    loop(lambda i: copy1(i).wait_send())
    loop(lambda i: copy2(i).wait_send())
    for i in range(1, kpts):
        copy3(i).wait_send()


def filter_kernel(slots, v_ref, smooth_ref, pot_ref, mh, ml, ty, tz, a1, b1, a2, b2, dy, dz,
                  mxh, mxl, mxth, mxtl, kx_ref, out_ref,
                  kxh, kxl, pair, first, vh, vl, jh, jl, ph, plo, wh, wl, nh, nl, ah, al, dh, dl):
    rows = NZ * NY
    for z in range(NZ):
        at = pl.ds(z * NY, NY)
        put_split((nh, nl), at, ty[...] * tz[z:z + 1, :])
        put_split((ah, al), at, a1[...] * b1[z:z + 1, :] + a2[...] * b2[z:z + 1, :])
        put_split((dh, dl), at, dy[...] * b1[z:z + 1, :] + a2[...] * dz[z:z + 1, :])
    kxh[...], kxl[...] = split(kx_ref[...])
    for y in range(NY):
        line = pot_ref[:, y * NX:(y + 1) * NX]
        pair[pl.ds(y, NZ, stride=NY), :] = line

    def wide_pair(at):
        return jnp.concatenate([pair[at, :]] * (2 * slots), axis=1)

    def prepare(at):
        high, low = split(v_ref[at, :])
        vh[at, :] = high
        vl[at, :] = low
        put_split((jh, jl), at, swap_lanes(v_ref[at, :], slots))
        put_split((ph, plo), at, smooth_ref[at, :] * wide_pair(at))

    tiles_of(rows, 160, prepare)

    def back(at):
        put_split((wh, wl), at, mm(nh[at, :], nl[at, :], ph[...], plo[...]))

    def kinetic_of(at):
        return (
            mm(vh[at, :], vl[at, :], kxh[...], kxl[...])
            + mm(wh[at, :], wl[at, :], mxth[...], mxtl[...])
            + mm(ah[at, :], al[at, :], vh[...], vl[...])
            + mm(dh[at, :], dl[at, :], jh[...], jl[...])
        )

    tiles_of(rows, TILE, back)

    def apply_first(at):
        first[at, :] = (kinetic_of(at) - spectrum_center * v_ref[at, :]) * (1.0 / spectrum_half)

    tiles_of(rows, TILE, apply_first)

    def prepare_again(at):
        x = first[at, :]
        high, low = split(x)
        vh[at, :] = high
        vl[at, :] = low
        put_split((jh, jl), at, swap_lanes(x, slots))
        put_split((wh, wl), at, mm(high, low, mxh[...], mxl[...]))

    tiles_of(rows, TILE, prepare_again)

    def smooth_again(at):
        s = mm(mh[at, :], ml[at, :], wh[...], wl[...])
        put_split((ph, plo), at, s * wide_pair(at))

    tiles_of(rows, TILE, smooth_again)
    tiles_of(rows, TILE, back)

    def finish(at):
        image = kinetic_of(at) - spectrum_center * first[at, :]
        out_ref[at, :] = (2.0 / spectrum_half) * image - v_ref[at, :]

    tiles_of(rows, TILE, finish)


def exchange_kernel(slots, ranks, cap, orbs, f_ref, off_ref, rows_ref, pick_ref, out_ref,
                    padded, send, recv, flat, gsend, grecv, s1, r1, s2, r2):
    o = lax.axis_index("orb")
    k = lax.axis_index("kpt")
    rows = NZ * NY
    count = slots * ranks
    barrier = pltpu.get_barrier_semaphore()

    def loop(f):
        def step(i, c):
            f(i)
            return c
        lax.fori_loop(1, ranks, step, 0)

    def peer(i):
        return lax.rem(o + i, ranks)

    loop(lambda i: pl.semaphore_signal(barrier, inc=1, device_id=(k, peer(i)), device_id_type=MESH))
    width = f_ref.shape[1]
    lane_tiles = -(-width // 128)
    block = lane_tiles * cap
    height = padded.shape[0] // lane_tiles
    for t in range(lane_tiles):
        used_lanes = min(128, width - t * 128)
        if used_lanes < 128:
            padded[t * height:t * height + rows, :] = jnp.zeros((rows, 128), jnp.float32)
        padded[t * height:t * height + rows, :used_lanes] = f_ref[:, t * 128:t * 128 + used_lanes]
        padded[t * height + rows:(t + 1) * height, :] = jnp.zeros((height - rows, 128), jnp.float32)

    def block_of(ref, d):
        return ref.at[pl.ds(pl.multiple_of(d * block, 8), block)]

    def put_window(ref, d):
        for t in range(lane_tiles):
            ref[pl.ds(d * block + t * cap, cap), :] = padded[pl.ds(off_ref[d] + t * height, cap), :]

    pl.semaphore_wait(barrier, ranks - 1)

    def copy(i, src, dst, sends, recvs):
        d = peer(i)
        return pltpu.make_async_remote_copy(
            src_ref=src(d), dst_ref=dst(o), send_sem=sends.at[d], recv_sem=recvs.at[o],
            device_id=(k, d), device_id_type=MESH)

    def arrived(i, dst, sends, recvs):
        d = peer(i)
        return pltpu.make_async_remote_copy(
            src_ref=dst(d), dst_ref=dst(d), send_sem=sends.at[d], recv_sem=recvs.at[d],
            device_id=(k, d), device_id_type=MESH)

    send_at = functools.partial(block_of, send)
    recv_at = functools.partial(block_of, recv)

    def gram_at(d):
        return grecv.at[d]

    def push(i):
        put_window(send, peer(i))
        copy(i, send_at, recv_at, s1, r1).start()

    loop(push)
    put_window(recv, o)
    loop(lambda i: arrived(i, recv_at, s1, r1).wait_recv())
    live = rows_ref[o]
    group = 4
    span = group * 2 * NX
    lane = lax.broadcasted_iota(jnp.int32, (count, span), 1)
    is_real = lax.rem(lane, 2 * NX) < NX

    def turned(x):
        return jnp.where(is_real, pltpu.roll(x, span - NX, 1), -pltpu.roll(x, NX, 1))

    def build(g, carry):
        real, imag = carry
        lines = []
        for j in range(group):
            r = g * group + j
            x3 = jnp.concatenate(
                [recv[pl.ds(t * cap + r, ranks, stride=block), :] for t in range(lane_tiles)], axis=1
            )
            line = jnp.concatenate([x3[:, s * 2 * NX:(s + 1) * 2 * NX] for s in range(slots)], axis=0)
            lines.append(line)
        x = jnp.concatenate(lines, axis=1)
        x = jnp.where(lane // (2 * NX) + g * group < live, x, 0.0)
        flat[:, pl.ds(pl.multiple_of(g * span, 128), span)] = x
        xh, xl = split(x)
        th, tl = split(turned(x))
        real = real + dot_nt(xh, xh) + dot_nt(xh, xl) + dot_nt(xl, xh)
        imag = imag + dot_nt(xh, th) + dot_nt(xh, tl) + dot_nt(xl, th)
        return real, imag

    zero = jnp.zeros((count, count), jnp.float32)
    real, imag = lax.fori_loop(0, cap // group, build, (zero, zero))
    ri = lax.broadcasted_iota(jnp.int32, (count, count), 0)
    ci = lax.broadcasted_iota(jnp.int32, (count, count), 1)
    packed = jnp.where(ri <= ci, real, imag)
    half = count // 2
    mine = jnp.concatenate([packed[:half], packed[half:]], axis=1)
    gsend[...] = mine
    grecv[o] = mine
    loop(lambda i: copy(i, lambda d: gsend, gram_at, s2, r2).start())
    loop(lambda i: arrived(i, gram_at, s2, r2).wait_recv())
    total = grecv[0]
    for j in range(1, ranks):
        total = total + grecv[j]
    packed = jnp.concatenate([total[:, :count], total[:, count:]], axis=0)
    other = packed.T
    real = jnp.where(ri <= ci, packed, other)
    imag = jnp.where(ri > ci, packed, jnp.where(ri < ci, -other, 0.0))
    pick = pick_ref[...]
    exact = functools.partial(jnp.dot, precision=exact_mode, preferred_element_type=jnp.float32)
    real_picked = exact(pick, real)
    imag_picked = exact(pick, imag)
    diagonal = jnp.sum(jnp.where(ri == ci, real, 0.0), axis=1, keepdims=True)
    trace = jnp.sum(exact(pick, jnp.broadcast_to(diagonal, (count, 128)))[:, :1])
    components = rows * 2 * NX
    mean_square = trace / (orbs * components) + 1e-06
    shrink = 0.5 / (components * mean_square)
    norm = 1.0 / jnp.sqrt(jnp.full((1, 1), mean_square, jnp.float32))
    used = jnp.sum(pick, axis=0, keepdims=True)
    rot_real = (1.5 * pick - shrink * real_picked * used) * norm
    rot_imag = (shrink * imag_picked * used) * norm
    rh, rl = split(rot_real)
    ih, il = split(rot_imag)

    def rotate(g, c):
        at = pl.ds(pl.multiple_of(g * span, 128), span)
        x = flat[:, at]
        xh, xl = split(x)
        th, tl = split(turned(x))
        out_ref[:, at] = mm(rh, rl, xh, xl) - mm(ih, il, th, tl)
        return c

    lax.fori_loop(0, cap // group, rotate, 0)
    loop(lambda i: copy(i, send_at, recv_at, s1, r1).wait_send())
    loop(lambda i: copy(i, lambda d: gsend, gram_at, s2, r2).wait_send())


def on_device(wavefunctions, kpoint_vector, kpoint_weight, occupation, orbital_slot, piece_rows,
              external_potential, core_density):
    f32 = jnp.float32
    slots = wavefunctions.shape[1]
    ranks = lax.axis_size("orb")
    kpts = lax.axis_size("kpt")
    own = lax.axis_index("orb")
    orbs = orbital_slot.shape[0]
    rows = NZ * NY
    cap = 2 * rows // ranks
    width = slots * 2 * NX
    slab = external_potential.shape[1]
    v = wavefunctions[0].reshape(slots, rows, 2 * NX).transpose(1, 0, 2).reshape(rows, width)
    wave_vector = kpoint_vector[0]
    offsets = jnp.cumsum(piece_rows) - piece_rows
    slot_ids = own * slots + jnp.arange(slots, dtype=jnp.int32)
    matches = (orbital_slot[:, None] == slot_ids[None, :]).astype(f32)
    weights = kpoint_weight[0] * jnp.sum(matches * occupation[:, None], axis=0)
    weights = jnp.repeat(weights, 2 * NX)[None, :]
    place = (orbital_slot % slots) * ranks + orbital_slot // slots
    pick = (place[:, None] == jnp.arange(slots * ranks, dtype=jnp.int32)[None, :]).astype(f32)
    first, second, mx, mxt, kx = tables(slots, wave_vector)
    sds = jax.ShapeDtypeStruct
    big = lambda n, w: [pltpu.VMEM((rows, w), BF)] * n
    dma = pltpu.SemaphoreType.DMA
    smooth, part, mh, ml = pl.pallas_call(
        functools.partial(smooth_kernel, slots),
        out_shape=[sds((rows, width), f32), sds((NZ, NY * NX), f32), sds((rows, rows), BF),
                   sds((rows, rows), BF)],
        in_specs=[VMEM] * 6, out_specs=[VMEM] * 4,
        scratch_shapes=big(2, width) + [pltpu.VMEM((rows, NX), f32)],
        name="smooth",
    )(v, *first, *mx, weights)
    every = kpts * ranks
    planes = NZ // kpts
    density, potential = pl.pallas_call(
        functools.partial(density_kernel, kpts, ranks),
        out_shape=[sds((NZ, slab), f32), sds((NZ, NY * NX), f32)],
        in_specs=[VMEM] * 3, out_specs=[VMEM] * 2,
        scratch_shapes=[pltpu.VMEM((every, planes, slab), f32)] * 2
        + [pltpu.VMEM((planes, slab), f32), pltpu.VMEM((every, planes, slab), f32),
           pltpu.VMEM((planes, slab), f32), pltpu.VMEM((kpts, planes, slab), f32)]
        + [dma((every,))] * 4 + [dma((kpts,))] * 2,
        compiler_params=pltpu.CompilerParams(collective_id=0, has_side_effects=True),
        name="density",
    )(part, external_potential, core_density)
    filtered = pl.pallas_call(
        functools.partial(filter_kernel, slots),
        out_shape=sds((rows, width), f32),
        in_specs=[VMEM] * 18, out_specs=VMEM,
        scratch_shapes=[pltpu.VMEM((width, width), BF)] * 2 + [pltpu.VMEM((rows, NX), f32), pltpu.VMEM((rows, width), f32)]
        + big(8, width) + big(6, rows),
        name="filter",
    )(v, smooth, potential, mh, ml, *second, *mx, *mxt, kx)
    count = slots * ranks
    lane_tiles = -(-width // 128)
    new_rows = pl.pallas_call(
        functools.partial(exchange_kernel, slots, ranks, cap, orbs),
        out_shape=sds((orbs, cap * 2 * NX), f32),
        in_specs=[VMEM, SMEM, SMEM, VMEM], out_specs=VMEM,
        scratch_shapes=[pltpu.VMEM((lane_tiles * (rows + (cap + 15) // 8 * 8), 128), f32)]
        + [pltpu.VMEM((ranks * lane_tiles * cap, 128), f32)] * 2
        + [pltpu.VMEM((count, cap * 2 * NX), f32), pltpu.VMEM((count // 2, 2 * count), f32),
           pltpu.VMEM((ranks, count // 2, 2 * count), f32)] + [dma((ranks,))] * 4,
        compiler_params=pltpu.CompilerParams(collective_id=1, has_side_effects=True),
        name="exchange",
    )(filtered, offsets, piece_rows, pick)
    return (density, new_rows[None])


def solution(mesh):
    in_specs = (
        P("kpt", "orb", None),
        P("kpt", None),
        P("kpt"),
        P(),
        P(),
        P(),
        P(None, "orb"),
        P(None, "orb"),
    )
    out_specs = (P(None, "orb"), P("kpt", None, "orb"))
    return jax.shard_map(
        on_device, mesh=mesh, in_specs=in_specs, out_specs=out_specs, check_vma=False
    )
```

profile of v0, /device:TPU:0, one launch (start us, length us, event | category | flops | bytes accessed | tf_op | source)
XLA Modules:
  0.0 173.1 jit_solution(15561188300294960505)
XLA Ops:
  0.6 5.8 %reduce.1 = f32[3,102400]{1,0:T(4,128)} reduce(f32[1,3,102400]{2,0,1:T(1,128)} %param.24, f32[]{:T(128)} %constant.86), dimensions={0}, to_apply=%param.24.reduce_sub_computation | reduce | bytes 2457604 | tf_op args[0]
  6.4 2.7 %reshape_squeeze.3 = f32[3,640,160]{2,1,0:T(8,128)S(1)} reshape(f32[3,102400]{1,0:T(4,128)} %reduce.1) | data formatting | bytes 2457600 | tf_op jit(solution)/shard_map/reshape;squeeze | solution.py:500
  9.1 1.3 copy.32
  10.4 0.0 copy-start.7
  10.4 0.0 copy-start.8
  10.4 1.5 copy.33.v_ref
  11.9 0.0 copy-done.7
  11.9 0.0 copy-done.8
  11.9 0.2 select_reduce_fusion
  12.7 0.1 broadcast_in_dim.4
  12.8 0.7 broadcast_in_dim_reshape.3.w_ref
  13.5 0.0 copy-start.5
  13.5 0.0 copy-start.2
  13.5 0.0 copy-start.3
  13.5 0.0 copy-start
  13.5 0.0 copy-start.1
  13.5 7.5 %smooth.1 = (f32[640,480]{1,0:T(8,128)}, f32[8,6400]{1,0:T(8,128)}, bf16[640,640]{1,0:T(8,128)(2,1)}, bf16[640,640]{1,0:T(8,128)(2,1)}) custom-call(f32[640,480]{1,0:T(8,128)} %copy.33.v_ref, f32[80,640]{1,0:T(8,128)} %constant.71.clone.my, f32[8,640]{1,0:T(8,128)} %constant.72.clone.mz, bf16[480,480]{1,0:T(8,128)(2,1)} %constant.73.clone.mxh, ...), custom_call_target="tpu_custom_call" | custom-call | tf_op jit(solution)/shard_map/smooth/pallas_call | solution.py:513
  21.0 25.8 %density.1 = (f32[8,400]{1,0:T(8,128)}, f32[8,6400]{1,0:T(8,128)}) custom-call(f32[8,6400]{1,0:T(8,128)} %get-tuple-element.8.part_ref, f32[8,400]{1,0:T(8,128)} %ext_ref.1, f32[8,400]{1,0:T(8,128)} %core_ref.1), custom_call_target="tpu_custom_call" | custom-call | tf_op jit(solution)/shard_map/density/pallas_call | solution.py:523
  46.8 0.0 copy-done.5
  46.8 0.7 fusion.3
  47.5 0.0 copy-done.2
  47.5 1.3 broadcast_multiply_fusion.dy
  48.8 0.0 copy-done.3
  48.8 1.3 broadcast_multiply_fusion.1.dz
  50.1 0.7 multiply_reduce_fusion
  51.4 0.0 copy-done
  51.5 0.0 copy-done.1
  51.5 1.9 %add_add_fusion.kx_ref = f32[480,480]{1,0:T(8,128)} fusion(f32[480,480]{1,0:T(8,128)S(1)} %copy-done, f32[480,480]{1,0:T(8,128)S(1)} %copy-done.1, f32[]{:T(128)S(6)} %mul_shard_map.3, f32[]{:T(128)} %bitcast.5), kind=kLoop, calls=%fused_computation | loop fusion | flops 1152000 | bytes 2764808 | tf_op jit(solution)/shard_map/add | solution.py:134
  53.3 0.0 copy-start.6
  53.3 25.9 %filter.1.f_ref = f32[640,480]{1,0:T(8,128)} custom-call(f32[640,480]{1,0:T(8,128)} %copy.33.v_ref, f32[640,480]{1,0:T(8,128)} %get-tuple-element.10.smooth_ref, f32[8,6400]{1,0:T(8,128)} %get-tuple-element.11.pot_ref, bf16[640,640]{1,0:T(8,128)(2,1)} %get-tuple-element.12.mh, bf16[640,640]{1,0:T(8,128)(2,1)} %get-tuple-element.13.ml, ...), custom_call_target="tpu_custom_call" | custom-call | tf_op jit(solution)/shard_map/filter/pallas_call | solution.py:534
  79.2 0.0 copy-done.6
  79.2 0.1 copy.35
  79.3 0.1 reduce.2
  79.4 0.5 sub.9.off_ref
  80.0 0.7 fusion.pick_ref
  80.7 0.0 copy-start.4
  80.7 88.6 %exchange.1 = f32[48,12800]{1,0:T(8,128)} custom-call(f32[640,480]{1,0:T(8,128)} %filter.1.f_ref, s32[16]{0:T(128)} %sub.9.off_ref, s32[16]{0:T(128)} %rows_ref.1, f32[48,48]{1,0:T(8,128)} %fusion.pick_ref), custom_call_target="tpu_custom_call" | custom-call | tf_op jit(solution)/shard_map/exchange/pallas_call | solution.py:544
  169.2 0.0 copy-done.4
  169.2 0.6 copy.39
  169.9 3.3 %copy.40 = f32[1,48,12800]{2,1,0:T(8,128)} copy(f32[1,48,12800]{2,1,0:T(8,128)} %bitcast.9) | data formatting | bytes 4915200
  (4 shorter events, 0.1 us)
Async XLA Ops:
  10.4 1.5 copy-start.7
  10.4 1.5 copy-start.8
  13.5 33.3 %copy-start.5 = (f32[1,3]{1,0:T(1,128)S(1)}, f32[1,3]{1,0:T(1,128)}, u32[]{:S(2)}) copy-start(f32[1,3]{1,0:T(1,128)} %param.25) | copy-start | bytes 40
  13.5 34.0 %copy-start.2 = (f32[80,640]{1,0:T(8,128)S(1)}, f32[80,640]{1,0:T(8,128)}, u32[]{:S(2)}) copy-start(f32[80,640]{1,0:T(8,128)} %constant.69.clone) | copy-start | bytes 614404
  13.5 35.3 %copy-start.3 = (f32[8,640]{1,0:T(8,128)S(1)}, f32[8,640]{1,0:T(8,128)}, u32[]{:S(2)}) copy-start(f32[8,640]{1,0:T(8,128)} %constant.70.clone) | copy-start | bytes 61444
  13.5 38.0 %copy-start = (f32[480,480]{1,0:T(8,128)S(1)}, f32[480,480]{1,0:T(8,128)}, u32[]{:S(2)}) copy-start(f32[480,480]{1,0:T(8,128)} %constant.67.clone) | copy-start | bytes 2764804
  13.5 38.0 %copy-start.1 = (f32[480,480]{1,0:T(8,128)S(1)}, f32[480,480]{1,0:T(8,128)}, u32[]{:S(2)}) copy-start(f32[480,480]{1,0:T(8,128)} %constant.68.clone) | copy-start | bytes 2764804
  53.3 25.9 %copy-start.6 = (s32[16]{0:T(128)S(1)}, s32[16]{0:T(128)}, u32[]{:S(2)}) copy-start(s32[16]{0:T(128)} %rows_ref.1) | copy-start | bytes 196
  80.7 88.6 %copy-start.4 = (f32[8,400]{1,0:T(8,128)S(1)}, f32[8,400]{1,0:T(8,128)}, u32[]{:S(2)}) copy-start(f32[8,400]{1,0:T(8,128)} %get-tuple-element.19) | copy-start | bytes 38404
where the time goes:
time: 173 us
  Pallas kernels  148 us (86%)
  other arithmetic  12.5 us (7%)
  local copies, waits for them, and re-layouts  10.8 us (6%)
  between operations  2.09 us (1%)
    pallas_call x1, Pallas kernels, on_device(): pl.pallas_call(functools.partial(exchange_kernel, slots, ranks, cap, orbs...  88.6 us
    pallas_call x1, Pallas kernels, on_device(): pl.pallas_call(functools.partial(filter_kernel, slots), out_shape=sds((ro...  25.9 us
    pallas_call x1, Pallas kernels, on_device(): pl.pallas_call(functools.partial(density_kernel, kpts, ranks), out_shape=...  25.8 us
    pallas_call x1, Pallas kernels, on_device(): pl.pallas_call(functools.partial(smooth_kernel, slots), out_shape=[sds((r...  7.49 us
    unnamed x1, other arithmetic  5.78 us
    unnamed x20, local copies, waits for them, and re-layouts  3.94 us

commit v1 on v0

--- a/solution.py
+++ b/solution.py
@@ -89,11 +89,6 @@
     return high, (x - high.astype(jnp.float32)).astype(BF)
 
 
-def split_table(x):
-    high = x.astype(BF)
-    return high, (x - high.astype(np.float32)).astype(BF)
-
-
 def dot(a, b):
     return lax.dot_general(a, b, (((1,), (0,)), ((), ())), preferred_element_type=jnp.float32)
 
@@ -119,29 +114,21 @@
     refs[1][at, :] = low
 
 
-def tables(slots, wave_vector):
+def tables():
     d2, d1, magic = axis_tables(NX)
     d2z, d1z, magic_z = axis_tables(NZ)
     d2y, d1y, magic_y = axis_tables(NY)
     f = lambda m: np.asarray(m, np.float32)
     wide = lambda m: f(np.tile(m, (1, NZ)))
     tall = lambda m: f(np.repeat(m, NY, axis=1))
-    eye = np.eye(2 * slots)
-    magic_x = split_table(f(np.kron(eye, magic.T)))
-    magic_xt = split_table(f(np.kron(eye, magic)))
+    pair = np.eye(2)
     twist = np.array([[0.0, 1.0], [-1.0, 0.0]])
-    along_x = (
-        jnp.asarray(f(np.kron(eye, d2.T)))
-        + wave_vector[0] * jnp.asarray(f(np.kron(np.eye(slots), np.kron(twist, d1).T)))
-        + 0.5 * jnp.sum(wave_vector * wave_vector) * jnp.eye(2 * slots * NX, dtype=jnp.float32)
-    )
-    first = [wide(magic_y), tall(magic_z)]
-    second = [
-        wide(magic_y.T), tall(magic_z.T),
-        wide(d2y), tall(np.eye(NZ)), wide(np.eye(NY)), tall(d2z),
-        wave_vector[1] * jnp.asarray(wide(d1y)), wave_vector[2] * jnp.asarray(tall(d1z)),
+    return [
+        wide(magic_y), tall(magic_z), wide(magic_y.T), tall(magic_z.T),
+        wide(d2y), tall(np.eye(NZ)), wide(np.eye(NY)), tall(d2z), wide(d1y), tall(d1z),
+        f(np.kron(pair, magic.T)), f(np.kron(pair, magic)),
+        f(np.kron(pair, d2.T)), f(np.kron(twist, d1).T),
     ]
-    return first, second, magic_x, magic_xt, along_x
 
 
 def tiles_of(rows, tile, body):
@@ -153,40 +140,26 @@
 
 
 TILE = 320
-
-
-def smooth_kernel(slots, v_ref, my, mz, mxh, mxl, w_ref, smooth_ref, part_ref, mh_out, ml_out,
-                  th, tl, dens):
+CHUNKS = 5
+
+
+def place_diagonal(refs, block, slots):
+    size = block.shape[0]
+    for n in range(slots):
+        parts = [jnp.zeros((size, n * size), jnp.float32)] * (n > 0) + [block]
+        if n < slots - 1:
+            parts.append(jnp.zeros((size, (slots - 1 - n) * size), jnp.float32))
+        put_split(refs, pl.ds(n * size, size), jnp.concatenate(parts, axis=1))
+
+
+def field_kernel(slots, kpts, ranks, wf_ref, occ_ref, slot_ref, q_ref, kw_ref, ext_ref, core_ref,
+                 my, mz, ty, tz, a1, b1, a2, b2, dy, dz, mx, mxt, kx0, kx1, dens_ref, out_ref,
+                 vt, v_ref, smooth_ref, part_ref, dens, pot_ref, pair, first,
+                 mh, ml, nh, nl, ah, al, dh, dl, mxh, mxl, mxth, mxtl, kxh, kxl,
+                 vh, vl, jh, jl, ph, plo, wh, wl,
+                 send1, recv1, send2, recv2, own_d, recv_d, s1, r1, s2, r2, s3, r3):
     rows = NZ * NY
-    for z in range(NZ):
-        block = my[...] * mz[z:z + 1, :]
-        put_split((mh_out, ml_out), pl.ds(z * NY, NY), block)
-
-    def along(at):
-        vh, vl = split(v_ref[at, :])
-        put_split((th, tl), at, mm(vh, vl, mxh[...], mxl[...]))
-
-    tiles_of(rows, TILE, along)
-
-    def across(at):
-        s = mm(mh_out[at, :], ml_out[at, :], th[...], tl[...])
-        smooth_ref[at, :] = s
-        q = s * s * w_ref[...]
-        total = q[:, :NX]
-        for i in range(1, 2 * slots):
-            total = total + q[:, i * NX:(i + 1) * NX]
-        dens[at, :] = total
-
-    tiles_of(rows, TILE, across)
-    group = 8
-    for g in range(NY // group):
-        part_ref[:, g * group * NX:(g + 1) * group * NX] = jnp.concatenate(
-            [dens[pl.ds(g * group + y, NZ, stride=NY), :] for y in range(group)], axis=1
-        )
-
-
-def density_kernel(kpts, ranks, part_ref, ext_ref, core_ref, dens_ref, pot_ref,
-                   send1, recv1, send2, recv2, own_d, recv_d, s1, r1, s2, r2, s3, r3):
+    full = slots * 2 * NX
     k = lax.axis_index("kpt")
     o = lax.axis_index("orb")
     every = kpts * ranks
@@ -205,6 +178,62 @@
         return c
 
     lax.fori_loop(1, every, greet, 0)
+
+    gather = 4
+    lines = gather * 2 * NX // 128
+    groups = rows // gather
+    lane_tiles = -(-full // 128)
+    for m in range(gather):
+        parts = []
+        for n in range(slots):
+            start, stop = m * 2 * NX, (m + 1) * 2 * NX
+            while start < stop:
+                j = start // 128
+                end = min(stop, (j + 1) * 128)
+                x = wf_ref[pl.ds(n * groups * lines + j, groups, stride=lines), :]
+                parts.append(x[:, start - j * 128:end - j * 128])
+                start = end
+        if lane_tiles * 128 > full:
+            parts.append(jnp.zeros((groups, lane_tiles * 128 - full), jnp.float32))
+        x = jnp.concatenate(parts, axis=1)
+        for t in range(lane_tiles):
+            vt[pl.ds(t * rows + m, groups, stride=gather), :] = x[:, t * 128:(t + 1) * 128]
+    for t in range(lane_tiles):
+        used = min(128, full - t * 128)
+        v_ref[:, t * 128:t * 128 + used] = vt[t * rows:(t + 1) * rows, :used]
+    for z in range(NZ):
+        put_split((mh, ml), pl.ds(z * NY, NY), my[...] * mz[z:z + 1, :])
+    place_diagonal((mxh, mxl), mx[...], slots)
+    loads = [
+        kw_ref[0] * jnp.sum(jnp.where(slot_ref[...] == o * slots + n, occ_ref[...], 0.0), axis=1,
+                            keepdims=True)
+        for n in range(slots)
+    ]
+
+    def along(at):
+        high, low = split(v_ref[at, :])
+        vh[at, :] = high
+        vl[at, :] = low
+        put_split((wh, wl), at, mm(high, low, mxh[...], mxl[...]))
+
+    tiles_of(rows, TILE, along)
+
+    def across(at):
+        x = mm(mh[at, :], ml[at, :], wh[...], wl[...])
+        smooth_ref[at, :] = x
+        total = jnp.zeros((TILE, NX), jnp.float32)
+        for n in range(slots):
+            re = x[:, 2 * n * NX:(2 * n + 1) * NX]
+            im = x[:, (2 * n + 1) * NX:(2 * n + 2) * NX]
+            total = total + loads[n] * (re * re + im * im)
+        dens[at, :] = total
+
+    tiles_of(rows, TILE, across)
+    group = 8
+    for g in range(NY // group):
+        part_ref[:, g * group * NX:(g + 1) * group * NX] = jnp.concatenate(
+            [dens[pl.ds(g * group + y, NZ, stride=NY), :] for y in range(group)], axis=1
+        )
     for j in range(every):
         a, b = divmod(j, ranks)
         send1[j] = part_ref[a * planes:(a + 1) * planes, b * width:(b + 1) * width]
@@ -242,6 +271,25 @@
 
     loop(lambda i: copy1(i).start())
     recv1[me] = send1[me]
+
+    for z in range(NZ):
+        at = pl.ds(z * NY, NY)
+        put_split((nh, nl), at, ty[...] * tz[z:z + 1, :])
+        put_split((ah, al), at, a1[...] * b1[z:z + 1, :] + a2[...] * b2[z:z + 1, :])
+        put_split((dh, dl), at, dy[...] * (q_ref[0, 1] * b1[z:z + 1, :])
+                  + a2[...] * (q_ref[0, 2] * dz[z:z + 1, :]))
+    place_diagonal((mxth, mxtl), mxt[...], slots)
+    half_q2 = 0.5 * (q_ref[0, 0] * q_ref[0, 0] + q_ref[0, 1] * q_ref[0, 1] + q_ref[0, 2] * q_ref[0, 2])
+    eye = (lax.broadcasted_iota(jnp.int32, (2 * NX, 2 * NX), 0)
+           == lax.broadcasted_iota(jnp.int32, (2 * NX, 2 * NX), 1))
+    along_x = kx0[...] + q_ref[0, 0] * kx1[...] + jnp.where(eye, half_q2, 0.0)
+    place_diagonal((kxh, kxl), along_x, slots)
+
+    def twist(at):
+        put_split((jh, jl), at, swap_lanes(v_ref[at, :], slots))
+
+    tiles_of(rows, 160, twist)
+
     loop(lambda i: arrived(i, recv1, s1, r1).wait_recv())
     total = recv1[0]
     for j in range(1, every):
@@ -262,6 +310,18 @@
     loop(lambda i: copy2(i).start())
     for i in range(1, kpts):
         copy3(i).start()
+
+    def kinetic_of(at):
+        return (
+            mm(vh[at, :], vl[at, :], kxh[...], kxl[...])
+            + mm(ah[at, :], al[at, :], vh[...], vl[...])
+            + mm(dh[at, :], dl[at, :], jh[...], jl[...])
+        )
+
+    def begin(at):
+        first[at, :] = kinetic_of(at) - spectrum_center * v_ref[at, :]
+
+    tiles_of(rows, TILE, begin)
     loop(lambda i: arrived(i, recv2, s2, r2).wait_recv())
     for j in range(every):
         a, b = divmod(j, ranks)
@@ -277,71 +337,48 @@
     loop(lambda i: copy2(i).wait_send())
     for i in range(1, kpts):
         copy3(i).wait_send()
-
-
-def filter_kernel(slots, v_ref, smooth_ref, pot_ref, mh, ml, ty, tz, a1, b1, a2, b2, dy, dz,
-                  mxh, mxl, mxth, mxtl, kx_ref, out_ref,
-                  kxh, kxl, pair, first, vh, vl, jh, jl, ph, plo, wh, wl, nh, nl, ah, al, dh, dl):
-    rows = NZ * NY
-    for z in range(NZ):
-        at = pl.ds(z * NY, NY)
-        put_split((nh, nl), at, ty[...] * tz[z:z + 1, :])
-        put_split((ah, al), at, a1[...] * b1[z:z + 1, :] + a2[...] * b2[z:z + 1, :])
-        put_split((dh, dl), at, dy[...] * b1[z:z + 1, :] + a2[...] * dz[z:z + 1, :])
-    kxh[...], kxl[...] = split(kx_ref[...])
     for y in range(NY):
-        line = pot_ref[:, y * NX:(y + 1) * NX]
-        pair[pl.ds(y, NZ, stride=NY), :] = line
+        pair[pl.ds(y, NZ, stride=NY), :] = pot_ref[:, y * NX:(y + 1) * NX]
 
     def wide_pair(at):
         return jnp.concatenate([pair[at, :]] * (2 * slots), axis=1)
 
-    def prepare(at):
-        high, low = split(v_ref[at, :])
-        vh[at, :] = high
-        vl[at, :] = low
-        put_split((jh, jl), at, swap_lanes(v_ref[at, :], slots))
+    def weigh(at):
         put_split((ph, plo), at, smooth_ref[at, :] * wide_pair(at))
 
-    tiles_of(rows, 160, prepare)
+    tiles_of(rows, 160, weigh)
 
     def back(at):
         put_split((wh, wl), at, mm(nh[at, :], nl[at, :], ph[...], plo[...]))
 
-    def kinetic_of(at):
-        return (
-            mm(vh[at, :], vl[at, :], kxh[...], kxl[...])
-            + mm(wh[at, :], wl[at, :], mxth[...], mxtl[...])
-            + mm(ah[at, :], al[at, :], vh[...], vl[...])
-            + mm(dh[at, :], dl[at, :], jh[...], jl[...])
-        )
+    def potential_of(at):
+        return mm(wh[at, :], wl[at, :], mxth[...], mxtl[...])
 
     tiles_of(rows, TILE, back)
 
     def apply_first(at):
-        first[at, :] = (kinetic_of(at) - spectrum_center * v_ref[at, :]) * (1.0 / spectrum_half)
-
-    tiles_of(rows, TILE, apply_first)
-
-    def prepare_again(at):
-        x = first[at, :]
+        x = (first[at, :] + potential_of(at)) * (1.0 / spectrum_half)
+        first[at, :] = x
         high, low = split(x)
         vh[at, :] = high
         vl[at, :] = low
         put_split((jh, jl), at, swap_lanes(x, slots))
-        put_split((wh, wl), at, mm(high, low, mxh[...], mxl[...]))
+
+    tiles_of(rows, 160, apply_first)
+
+    def prepare_again(at):
+        put_split((wh, wl), at, mm(vh[at, :], vl[at, :], mxh[...], mxl[...]))
 
     tiles_of(rows, TILE, prepare_again)
 
     def smooth_again(at):
-        s = mm(mh[at, :], ml[at, :], wh[...], wl[...])
-        put_split((ph, plo), at, s * wide_pair(at))
+        put_split((ph, plo), at, mm(mh[at, :], ml[at, :], wh[...], wl[...]) * wide_pair(at))
 
     tiles_of(rows, TILE, smooth_again)
     tiles_of(rows, TILE, back)
 
     def finish(at):
-        image = kinetic_of(at) - spectrum_center * first[at, :]
+        image = kinetic_of(at) + potential_of(at) - spectrum_center * first[at, :]
         out_ref[at, :] = (2.0 / spectrum_half) * image - v_ref[at, :]
 
     tiles_of(rows, TILE, finish)
@@ -367,7 +404,9 @@
     loop(lambda i: pl.semaphore_signal(barrier, inc=1, device_id=(k, peer(i)), device_id_type=MESH))
     width = f_ref.shape[1]
     lane_tiles = -(-width // 128)
-    block = lane_tiles * cap
+    parts = CHUNKS
+    chunk = cap // parts
+    block = lane_tiles * chunk
     height = padded.shape[0] // lane_tiles
     for t in range(lane_tiles):
         used_lanes = min(128, width - t * 128)
@@ -376,40 +415,49 @@
         padded[t * height:t * height + rows, :used_lanes] = f_ref[:, t * 128:t * 128 + used_lanes]
         padded[t * height + rows:(t + 1) * height, :] = jnp.zeros((height - rows, 128), jnp.float32)
 
-    def block_of(ref, d):
-        return ref.at[pl.ds(pl.multiple_of(d * block, 8), block)]
-
-    def put_window(ref, d):
+    def block_of(ref, c, d):
+        return ref.at[pl.ds(pl.multiple_of((c * ranks + d) * block, 8), block)]
+
+    def put_window(ref, c, d):
         for t in range(lane_tiles):
-            ref[pl.ds(d * block + t * cap, cap), :] = padded[pl.ds(off_ref[d] + t * height, cap), :]
+            at = pl.ds((c * ranks + d) * block + t * chunk, chunk)
+            ref[at, :] = padded[pl.ds(off_ref[d] + c * chunk + t * height, chunk), :]
 
     pl.semaphore_wait(barrier, ranks - 1)
 
-    def copy(i, src, dst, sends, recvs):
+    def chunk_copy(c, i):
         d = peer(i)
         return pltpu.make_async_remote_copy(
-            src_ref=src(d), dst_ref=dst(o), send_sem=sends.at[d], recv_sem=recvs.at[o],
+            src_ref=block_of(send, c, d), dst_ref=block_of(recv, c, o),
+            send_sem=s1.at[c * ranks + d], recv_sem=r1.at[c * ranks + o],
             device_id=(k, d), device_id_type=MESH)
 
-    def arrived(i, dst, sends, recvs):
+    def chunk_arrived(c, i):
         d = peer(i)
         return pltpu.make_async_remote_copy(
-            src_ref=dst(d), dst_ref=dst(d), send_sem=sends.at[d], recv_sem=recvs.at[d],
+            src_ref=block_of(recv, c, d), dst_ref=block_of(recv, c, d),
+            send_sem=s1.at[c * ranks + d], recv_sem=r1.at[c * ranks + d],
             device_id=(k, d), device_id_type=MESH)
 
-    send_at = functools.partial(block_of, send)
-    recv_at = functools.partial(block_of, recv)
-
-    def gram_at(d):
-        return grecv.at[d]
-
-    def push(i):
-        put_window(send, peer(i))
-        copy(i, send_at, recv_at, s1, r1).start()
-
-    loop(push)
-    put_window(recv, o)
-    loop(lambda i: arrived(i, recv_at, s1, r1).wait_recv())
+    def copy(i):
+        d = peer(i)
+        return pltpu.make_async_remote_copy(
+            src_ref=gsend, dst_ref=grecv.at[o], send_sem=s2.at[d], recv_sem=r2.at[o],
+            device_id=(k, d), device_id_type=MESH)
+
+    def arrived(i):
+        d = peer(i)
+        return pltpu.make_async_remote_copy(
+            src_ref=grecv.at[d], dst_ref=grecv.at[d], send_sem=s2.at[d], recv_sem=r2.at[d],
+            device_id=(k, d), device_id_type=MESH)
+
+    for c in range(parts):
+        def push(i):
+            put_window(send, c, peer(i))
+            chunk_copy(c, i).start()
+
+        loop(push)
+        put_window(recv, c, o)
     live = rows_ref[o]
     group = 4
     span = group * 2 * NX
@@ -419,13 +467,14 @@
     def turned(x):
         return jnp.where(is_real, pltpu.roll(x, span - NX, 1), -pltpu.roll(x, NX, 1))
 
-    def build(g, carry):
+    def build(c, inner, carry):
         real, imag = carry
+        g = c * (chunk // group) + inner
         lines = []
         for j in range(group):
-            r = g * group + j
+            base = c * ranks * block + inner * group + j
             x3 = jnp.concatenate(
-                [recv[pl.ds(t * cap + r, ranks, stride=block), :] for t in range(lane_tiles)], axis=1
+                [recv[pl.ds(base + t * chunk, ranks, stride=block), :] for t in range(lane_tiles)], axis=1
             )
             line = jnp.concatenate([x3[:, s * 2 * NX:(s + 1) * 2 * NX] for s in range(slots)], axis=0)
             lines.append(line)
@@ -439,7 +488,10 @@
         return real, imag
 
     zero = jnp.zeros((count, count), jnp.float32)
-    real, imag = lax.fori_loop(0, cap // group, build, (zero, zero))
+    real = imag = zero
+    for c in range(parts):
+        loop(lambda i: chunk_arrived(c, i).wait_recv())
+        real, imag = lax.fori_loop(0, chunk // group, functools.partial(build, c), (real, imag))
     ri = lax.broadcasted_iota(jnp.int32, (count, count), 0)
     ci = lax.broadcasted_iota(jnp.int32, (count, count), 1)
     packed = jnp.where(ri <= ci, real, imag)
@@ -447,8 +499,8 @@
     mine = jnp.concatenate([packed[:half], packed[half:]], axis=1)
     gsend[...] = mine
     grecv[o] = mine
-    loop(lambda i: copy(i, lambda d: gsend, gram_at, s2, r2).start())
-    loop(lambda i: arrived(i, gram_at, s2, r2).wait_recv())
+    loop(lambda i: copy(i).start())
+    loop(lambda i: arrived(i).wait_recv())
     total = grecv[0]
     for j in range(1, ranks):
         total = total + grecv[j]
@@ -481,8 +533,9 @@
         return c
 
     lax.fori_loop(0, cap // group, rotate, 0)
-    loop(lambda i: copy(i, send_at, recv_at, s1, r1).wait_send())
-    loop(lambda i: copy(i, lambda d: gsend, gram_at, s2, r2).wait_send())
+    for c in range(parts):
+        loop(lambda i: chunk_copy(c, i).wait_send())
+    loop(lambda i: copy(i).wait_send())
 
 
 def on_device(wavefunctions, kpoint_vector, kpoint_weight, occupation, orbital_slot, piece_rows,
@@ -491,64 +544,48 @@
     slots = wavefunctions.shape[1]
     ranks = lax.axis_size("orb")
     kpts = lax.axis_size("kpt")
-    own = lax.axis_index("orb")
     orbs = orbital_slot.shape[0]
     rows = NZ * NY
     cap = 2 * rows // ranks
     width = slots * 2 * NX
     slab = external_potential.shape[1]
-    v = wavefunctions[0].reshape(slots, rows, 2 * NX).transpose(1, 0, 2).reshape(rows, width)
-    wave_vector = kpoint_vector[0]
+    lines = wavefunctions.reshape(slots * rows * 2 * NX // 128, 128)
     offsets = jnp.cumsum(piece_rows) - piece_rows
-    slot_ids = own * slots + jnp.arange(slots, dtype=jnp.int32)
-    matches = (orbital_slot[:, None] == slot_ids[None, :]).astype(f32)
-    weights = kpoint_weight[0] * jnp.sum(matches * occupation[:, None], axis=0)
-    weights = jnp.repeat(weights, 2 * NX)[None, :]
     place = (orbital_slot % slots) * ranks + orbital_slot // slots
     pick = (place[:, None] == jnp.arange(slots * ranks, dtype=jnp.int32)[None, :]).astype(f32)
-    first, second, mx, mxt, kx = tables(slots, wave_vector)
-    sds = jax.ShapeDtypeStruct
-    big = lambda n, w: [pltpu.VMEM((rows, w), BF)] * n
-    dma = pltpu.SemaphoreType.DMA
-    smooth, part, mh, ml = pl.pallas_call(
-        functools.partial(smooth_kernel, slots),
-        out_shape=[sds((rows, width), f32), sds((NZ, NY * NX), f32), sds((rows, rows), BF),
-                   sds((rows, rows), BF)],
-        in_specs=[VMEM] * 6, out_specs=[VMEM] * 4,
-        scratch_shapes=big(2, width) + [pltpu.VMEM((rows, NX), f32)],
-        name="smooth",
-    )(v, *first, *mx, weights)
+    consts = tables()
     every = kpts * ranks
     planes = NZ // kpts
-    density, potential = pl.pallas_call(
-        functools.partial(density_kernel, kpts, ranks),
-        out_shape=[sds((NZ, slab), f32), sds((NZ, NY * NX), f32)],
-        in_specs=[VMEM] * 3, out_specs=[VMEM] * 2,
-        scratch_shapes=[pltpu.VMEM((every, planes, slab), f32)] * 2
-        + [pltpu.VMEM((planes, slab), f32), pltpu.VMEM((every, planes, slab), f32),
-           pltpu.VMEM((planes, slab), f32), pltpu.VMEM((kpts, planes, slab), f32)]
+    lane_tiles = -(-width // 128)
+    vm = pltpu.VMEM
+    dma = pltpu.SemaphoreType.DMA
+    density, filtered = pl.pallas_call(
+        functools.partial(field_kernel, slots, kpts, ranks),
+        out_shape=[jax.ShapeDtypeStruct((NZ, slab), f32), jax.ShapeDtypeStruct((rows, width), f32)],
+        in_specs=[VMEM] * 3 + [SMEM] * 2 + [VMEM] * (2 + len(consts)), out_specs=[VMEM] * 2,
+        scratch_shapes=[vm((lane_tiles * rows, 128), f32), vm((rows, width), f32),
+                        vm((rows, width), f32), vm((NZ, NY * NX), f32), vm((rows, NX), f32),
+                        vm((NZ, NY * NX), f32), vm((rows, NX), f32), vm((rows, width), f32)]
+        + [vm((rows, rows), BF)] * 8 + [vm((width, width), BF)] * 6 + [vm((rows, width), BF)] * 8
+        + [vm((every, planes, slab), f32)] * 2
+        + [vm((planes, slab), f32), vm((every, planes, slab), f32),
+           vm((planes, slab), f32), vm((kpts, planes, slab), f32)]
         + [dma((every,))] * 4 + [dma((kpts,))] * 2,
         compiler_params=pltpu.CompilerParams(collective_id=0, has_side_effects=True),
-        name="density",
-    )(part, external_potential, core_density)
-    filtered = pl.pallas_call(
-        functools.partial(filter_kernel, slots),
-        out_shape=sds((rows, width), f32),
-        in_specs=[VMEM] * 18, out_specs=VMEM,
-        scratch_shapes=[pltpu.VMEM((width, width), BF)] * 2 + [pltpu.VMEM((rows, NX), f32), pltpu.VMEM((rows, width), f32)]
-        + big(8, width) + big(6, rows),
-        name="filter",
-    )(v, smooth, potential, mh, ml, *second, *mx, *mxt, kx)
+        name="field",
+    )(lines, occupation[None], orbital_slot[None], kpoint_vector, kpoint_weight,
+      external_potential, core_density, *consts)
     count = slots * ranks
     lane_tiles = -(-width // 128)
     new_rows = pl.pallas_call(
         functools.partial(exchange_kernel, slots, ranks, cap, orbs),
-        out_shape=sds((orbs, cap * 2 * NX), f32),
+        out_shape=jax.ShapeDtypeStruct((orbs, cap * 2 * NX), f32),
         in_specs=[VMEM, SMEM, SMEM, VMEM], out_specs=VMEM,
         scratch_shapes=[pltpu.VMEM((lane_tiles * (rows + (cap + 15) // 8 * 8), 128), f32)]
         + [pltpu.VMEM((ranks * lane_tiles * cap, 128), f32)] * 2
         + [pltpu.VMEM((count, cap * 2 * NX), f32), pltpu.VMEM((count // 2, 2 * count), f32),
-           pltpu.VMEM((ranks, count // 2, 2 * count), f32)] + [dma((ranks,))] * 4,
+           pltpu.VMEM((ranks, count // 2, 2 * count), f32)] + [dma((CHUNKS * ranks,))] * 2
+        + [dma((ranks,))] * 2,
         compiler_params=pltpu.CompilerParams(collective_id=1, has_side_effects=True),
         name="exchange",
     )(filtered, offsets, piece_rows, pick)

time: 173 us -> 136 us (0.79)
  Pallas kernels: 148 us -> 127 us
  other arithmetic: 12.5 us -> 2.68 us
  local copies, waits for them, and re-layouts: 10.8 us -> 4.63 us
    pallas_call x3 -> x1, Pallas kernels: 59.1 us -> 44.8 us  [on_device(): pl.pallas_call(functools.partial(field_kernel, slots, kpts, ranks), out_s...]
    pallas_call x1, Pallas kernels: 88.6 us -> 82.6 us  [on_device(): pl.pallas_call(functools.partial(exchange_kernel, slots, ranks, cap, orbs...]
    unnamed x1 -> x0, other arithmetic: 5.78 us -> none
    another operation x3 -> x1, local copies, waits for them, and re-layouts: 3.47 us -> 0.73 us  [the longest x1 2.72 us: on_device(): wavefunctions[0].reshape(slots, rows, 2 * NX).transpose(1, 0, 2)]
    mul x3 -> x0, other arithmetic: 2.61 us -> none  [the longest x1 1.31 us: tables(): wave_vector[1] * jnp.asarray(wide(d1y))]
    add x2 -> x0, other arithmetic: 1.85 us -> none  [the longest x1 1.85 us: tables(): jnp.asarray(f(np.kron(eye, d2.T)))]
    unnamed x20 -> x4, local copies, waits for them, and re-layouts: 3.94 us -> 3.9 us
where the time goes in v1:
time: 136 us
  Pallas kernels  127 us (93%)
  local copies, waits for them, and re-layouts  4.63 us (3%)
  other arithmetic  2.68 us (2%)
    pallas_call x1, Pallas kernels, on_device(): pl.pallas_call(functools.partial(exchange_kernel, slots, ranks, cap, orbs...  82.6 us
    pallas_call x1, Pallas kernels, on_device(): pl.pallas_call(functools.partial(field_kernel, slots, kpts, ranks), out_s...  44.8 us
    unnamed x4, local copies, waits for them, and re-layouts  3.9 us

profile of v1, /device:TPU:0, one launch (start us, length us, event | category | flops | bytes accessed | tf_op | source)
XLA Modules:
  0.0 136.0 jit_solution(2050337054037358592)
XLA Ops:
  1.3 0.7 fusion.2
  1.9 0.7 copy.25
  2.7 0.1 reduce
  2.8 1.2 sub.9.off_ref
  4.0 0.7 fusion.pick_ref
  4.7 44.8 %field.1 = (f32[8,400]{1,0:T(8,128)}, f32[640,480]{1,0:T(8,128)}) custom-call(f32[2400,128]{1,0:T(8,128)} %bitcast.6, f32[1,48]{1,0:T(1,128)} %bitcast.8, s32[1,48]{1,0:T(1,128)} %bitcast.9, f32[1,3]{1,0:T(1,128)} %q_ref.1, f32[1]{0:T(128)S(6)} %copy.28.kw_ref, f32[8,400]{1,0:T(8,128)} %ext_ref.1, f32[8,400]{1,0:T(8,128)} %core_ref.1, ...), custom_call_target="tpu_custom_call" | custom-call | tf_op jit(solution)/shard_map/field/pallas_call | solution.py:562
  49.5 0.0 copy-start
  49.5 82.6 %exchange.1 = f32[48,12800]{1,0:T(8,128)} custom-call(f32[640,480]{1,0:T(8,128)} %get-tuple-element.5.f_ref, s32[16]{0:T(128)} %sub.9.off_ref, s32[16]{0:T(128)} %rows_ref.1, f32[48,48]{1,0:T(8,128)} %fusion.pick_ref), custom_call_target="tpu_custom_call" | custom-call | tf_op jit(solution)/shard_map/exchange/pallas_call | solution.py:580
  132.1 0.0 copy-done
  132.1 0.6 copy.29
  132.7 3.3 %copy.30 = f32[1,48,12800]{2,1,0:T(8,128)} copy(f32[1,48,12800]{2,1,0:T(8,128)} %bitcast.5) | data formatting | bytes 4915200
  (1 shorter events, 0.0 us)
Async XLA Ops:
  49.5 82.6 %copy-start = (f32[8,400]{1,0:T(8,128)S(1)}, f32[8,400]{1,0:T(8,128)}, u32[]{:S(2)}) copy-start(f32[8,400]{1,0:T(8,128)} %get-tuple-element.8) | copy-start | bytes 38404
